TPU v7x, 32 devices: a whole 2x2x4 slice. The times are simulated.
32 devices in a mesh: dp: 8 (over z, core), tensor: 4 (over y, x).
Axes of the slice: x: 2, y: 2, z: 4, core: 2. Of those that a mesh axis runs over, the one named last changes fastest.
Arguments:
- layer_input: bfloat16 [16384, 1024], P(('dp', 'tensor')), may hold values from -6 to 6
- segment_ids: int32 [32, 512], P('dp'), may hold values from 0 to 15, never falling along the last dimension, each value on 1 to 256 neighbouring positions
- w_qkv: bfloat16 [3, 1024, 1024], P(None, None, 'tensor'), may hold values from -0.1875 to 0.1875
- b_qv: bfloat16 [2, 1024], P(None, 'tensor'), may hold values from -3 to 3
- w_out: bfloat16 [1024, 1024], P('tensor'), may hold values from -0.5 to 0.5
- b_out: bfloat16 [1024], replicated, may hold values from -3 to 3
- ln1_gain: float32 [1024], replicated, may hold values from 0.5 to 1.5
- ln1_bias: float32 [1024], replicated, may hold values from -2 to 2
- w_up: bfloat16 [1024, 4096], P(None, 'tensor'), may hold values from -0.1875 to 0.1875
- b_up: bfloat16 [4096], P('tensor'), may hold values from -3 to 3
- w_down: bfloat16 [4096, 1024], P('tensor'), may hold values from -0.09375 to 0.09375
- b_down: bfloat16 [1024], replicated, may hold values from -2 to 2
- ln2_gain: float32 [1024], replicated, may hold values from 0.5 to 1.5
- ln2_bias: float32 [1024], replicated, may hold values from -2 to 2
- cotangent: bfloat16 [16384, 1024], P(('dp', 'tensor')), may hold values from -6 to 6
Outputs:
- output: bfloat16 [16384, 1024], P(('dp', 'tensor'))
- grad_input: float32 [16384, 1024], P(('dp', 'tensor'))
- grad_w_qkv: float32 [3, 1024, 1024], P(None, None, 'tensor')
- grad_b_qv: float32 [2, 1024], P(None, 'tensor')
- grad_w_out: float32 [1024, 1024], P('tensor')
- grad_b_out: float32 [1024], replicated
- grad_ln1_gain: float32 [1024], replicated
- grad_ln1_bias: float32 [1024], replicated
- grad_w_up: float32 [1024, 4096], P(None, 'tensor')
- grad_b_up: float32 [4096], P('tensor')
- grad_w_down: float32 [4096, 1024], P('tensor')
- grad_b_down: float32 [1024], replicated
- grad_ln2_gain: float32 [1024], replicated
- grad_ln2_bias: float32 [1024], replicated
Inputs may be any that keep to these rules, and one draw needn't show every extreme that they name: `segment_ids`: within a sequence the ids never fall; a document has at most 256 tokens.
All inputs are finite; a program needn't handle non-finite values.
Results may differ from a plain program's by a relative error of at most 0.018.
Values may be sent and summed in bfloat16 or wider, within the bound.
No kernel may reach another device: no remote copies, remote signals or barrier semaphores. Data moves between devices by JAX's collectives and lax.ppermute only.
A program may use at most 128 MiB of HBM per device.

v0:
```python
import jax
import jax.numpy as jnp
from jax import lax
from jax.sharding import PartitionSpec as P

HEAD_DIM = 64
norm_epsilon = 1e-05
root_half = 0.7071067811865476
inverse_root_two_pi = 0.3989422804014327


def layer_norm(token_rows, norm_gain, norm_bias):
    row_mean = jnp.mean(token_rows, -1, keepdims=True)
    centered = token_rows - row_mean
    variance = jnp.mean(centered * centered, -1, keepdims=True)
    inv_std = lax.rsqrt(variance + norm_epsilon)
    scaled = centered * inv_std
    return (scaled * norm_gain + norm_bias, scaled, inv_std)


def norm_back(incoming, scaled, inv_std, norm_gain):
    weighted = incoming * norm_gain
    d_rows = inv_std * (
        weighted
        - jnp.mean(weighted, -1, keepdims=True)
        - scaled * jnp.mean(weighted * scaled, -1, keepdims=True)
    )
    return (d_rows, jnp.sum(incoming * scaled, 0), jnp.sum(incoming, 0))


def gelu_value(up_proj):
    return 0.5 * up_proj * (1.0 + lax.erf(up_proj * root_half))


def gelu_slope(up_proj):
    return (
        0.5 * (1.0 + lax.erf(up_proj * root_half))
        + up_proj * jnp.exp(-0.5 * up_proj * up_proj) * inverse_root_two_pi
    )


def split_heads(matrix, head_count):
    return matrix.reshape(matrix.shape[0], head_count, -1)


def project(token_rows, w_qkv, b_qv):
    queries = (
        jnp.dot(token_rows, w_qkv[0], preferred_element_type=jnp.float32)
        + b_qv[0].astype(jnp.float32)
    ).astype(jnp.bfloat16)
    keys_low = jnp.dot(token_rows, w_qkv[1], preferred_element_type=jnp.float32).astype(
        jnp.bfloat16
    )
    values = (
        jnp.dot(token_rows, w_qkv[2], preferred_element_type=jnp.float32)
        + b_qv[1].astype(jnp.float32)
    ).astype(jnp.bfloat16)
    return (queries, keys_low, values)


def scores(queries, keys_low, segment, head_count, score_scale):
    raw = jnp.einsum(
        "qhd,khd->hqk",
        split_heads(queries, head_count),
        split_heads(keys_low, head_count),
        preferred_element_type=jnp.float32,
    )
    same_doc = segment[:, None] == segment[None, :]
    return jnp.where(same_doc[None], raw * score_scale, -1e30)


def mix_values(prob_low, values, head_count):
    context = jnp.einsum(
        "hqk,khd->qhd",
        prob_low,
        split_heads(values, head_count),
        preferred_element_type=jnp.float32,
    )
    return context.reshape(context.shape[0], -1).astype(jnp.bfloat16)


def ffn_forward(normed_low, up_weight, up_bias, down_weight):
    up_proj = jnp.dot(normed_low, up_weight, preferred_element_type=jnp.float32) + up_bias.astype(
        jnp.float32
    )
    activation = gelu_value(up_proj).astype(jnp.bfloat16)
    return jnp.dot(activation, down_weight, preferred_element_type=jnp.float32)


def ffn_backward(normed_low, branch_low, up_weight, up_bias, down_weight):
    up_proj = jnp.dot(normed_low, up_weight, preferred_element_type=jnp.float32) + up_bias.astype(
        jnp.float32
    )
    activation = gelu_value(up_proj).astype(jnp.bfloat16)
    grad_down = jnp.einsum("tf,td->fd", activation, branch_low, preferred_element_type=jnp.float32)
    d_activation = jnp.einsum(
        "td,fd->tf", branch_low, down_weight, preferred_element_type=jnp.float32
    )
    d_up = (d_activation * gelu_slope(up_proj)).astype(jnp.bfloat16)
    grad_up = jnp.einsum("td,tf->df", normed_low, d_up, preferred_element_type=jnp.float32)
    grad_up_bias = jnp.sum(d_up.astype(jnp.float32), 0)
    return (grad_up, grad_up_bias, grad_down, d_up)


def local(
    layer_input,
    segment_ids,
    w_qkv,
    b_qv,
    w_out,
    b_out,
    ln1_gain,
    ln1_bias,
    w_up,
    b_up,
    w_down,
    b_down,
    ln2_gain,
    ln2_bias,
    cotangent,
):
    my_rows, model_width = layer_input.shape
    seq_len = segment_ids.shape[1]
    score_scale = HEAD_DIM ** (-0.5)
    whole_input = lax.all_gather(layer_input, "tensor", axis=0, tiled=True)
    seq_input = whole_input.reshape(segment_ids.shape[0], seq_len, model_width)
    attn_width = w_out.shape[0]
    head_count = attn_width // HEAD_DIM

    def forward_seq(running, seq_item):
        token_rows, segment = seq_item
        queries, keys_low, values = project(token_rows, w_qkv, b_qv)
        logits = scores(queries, keys_low, segment, head_count, score_scale)
        row_max = jnp.max(logits, -1, keepdims=True)
        exponent = jnp.exp(logits - row_max)
        expo_sum = jnp.sum(exponent, -1, keepdims=True)
        prob_low = (exponent / expo_sum).astype(jnp.bfloat16)
        return (running, (mix_values(prob_low, values, head_count), row_max + jnp.log(expo_sum)))

    _, (seq_context, seq_lse) = lax.scan(forward_seq, None, (seq_input, segment_ids))
    all_context = seq_context.reshape(-1, attn_width)
    attention = lax.psum_scatter(
        jnp.dot(all_context, w_out, preferred_element_type=jnp.float32),
        "tensor",
        scatter_dimension=0,
        tiled=True,
    ) + b_out.astype(jnp.float32)
    normed_one, scaled_one, inv_one = layer_norm(
        layer_input.astype(jnp.float32) + attention, ln1_gain, ln1_bias
    )
    normed_low = normed_one.astype(jnp.bfloat16)
    whole_normed = lax.all_gather(normed_low, "tensor", axis=0, tiled=True)
    branch = lax.psum_scatter(
        ffn_forward(whole_normed, w_up, b_up, w_down), "tensor", scatter_dimension=0, tiled=True
    )
    normed_two, scaled_two, inv_two = layer_norm(
        normed_one + branch + b_down.astype(jnp.float32), ln2_gain, ln2_bias
    )
    d_second, grad_ln2_gain, grad_ln2_bias = norm_back(
        cotangent.astype(jnp.float32), scaled_two, inv_two, ln2_gain
    )
    branch_low = d_second.astype(jnp.bfloat16)
    grad_b_down = jnp.sum(branch_low.astype(jnp.float32), 0)
    whole_branch = lax.all_gather(branch_low, "tensor", axis=0, tiled=True)
    grad_w_up, grad_b_up, grad_w_down, d_up = ffn_backward(
        whole_normed, whole_branch, w_up, b_up, w_down
    )
    d_normed = lax.psum_scatter(
        jnp.einsum("tf,df->td", d_up, w_up, preferred_element_type=jnp.float32),
        "tensor",
        scatter_dimension=0,
        tiled=True,
    )
    d_first, grad_ln1_gain, grad_ln1_bias = norm_back(
        d_second + d_normed, scaled_one, inv_one, ln1_gain
    )
    attention_low = d_first.astype(jnp.bfloat16)
    grad_b_out = jnp.sum(attention_low.astype(jnp.float32), 0)
    whole_grad = lax.all_gather(attention_low, "tensor", axis=0, tiled=True)
    seq_grad = whole_grad.reshape(seq_input.shape[0], seq_len, model_width)

    def backward_seq(running, seq_item):
        grad_qkv, grad_bias, grad_out = running
        token_rows, segment, seq_lse_one, grad_rows = seq_item
        queries, keys_low, values = project(token_rows, w_qkv, b_qv)
        logits = scores(queries, keys_low, segment, head_count, score_scale)
        probability = jnp.exp(logits - seq_lse_one)
        prob_low = probability.astype(jnp.bfloat16)
        context = mix_values(prob_low, values, head_count)
        grad_out = grad_out + jnp.einsum(
            "te,td->ed", context, grad_rows, preferred_element_type=jnp.float32
        )
        d_context = jnp.einsum(
            "td,ed->te", grad_rows, w_out, preferred_element_type=jnp.float32
        ).astype(jnp.bfloat16)
        d_heads = split_heads(d_context, head_count)
        d_prob = jnp.einsum(
            "qhd,khd->hqk",
            d_heads,
            split_heads(values, head_count),
            preferred_element_type=jnp.float32,
        )
        d_values = (
            jnp.einsum("hqk,qhd->khd", prob_low, d_heads, preferred_element_type=jnp.float32)
            .reshape(seq_len, -1)
            .astype(jnp.bfloat16)
        )
        inner_sum = jnp.sum(probability * d_prob, -1, keepdims=True)
        d_raw = (probability * (d_prob - inner_sum) * score_scale).astype(jnp.bfloat16)
        d_queries = (
            jnp.einsum(
                "hqk,khd->qhd",
                d_raw,
                split_heads(keys_low, head_count),
                preferred_element_type=jnp.float32,
            )
            .reshape(seq_len, -1)
            .astype(jnp.bfloat16)
        )
        d_keys = (
            jnp.einsum(
                "hqk,qhd->khd",
                d_raw,
                split_heads(queries, head_count),
                preferred_element_type=jnp.float32,
            )
            .reshape(seq_len, -1)
            .astype(jnp.bfloat16)
        )
        grad_qkv = grad_qkv + jnp.stack(
            [
                jnp.einsum("td,te->de", token_rows, gradient, preferred_element_type=jnp.float32)
                for gradient in (d_queries, d_keys, d_values)
            ]
        )
        grad_bias = grad_bias + jnp.stack(
            [jnp.sum(d_queries.astype(jnp.float32), 0), jnp.sum(d_values.astype(jnp.float32), 0)]
        )
        return ((grad_qkv, grad_bias, grad_out), (d_queries, d_keys, d_values))

    start_grads = (
        jnp.zeros((3, model_width, attn_width), jnp.float32),
        jnp.zeros((2, attn_width), jnp.float32),
        jnp.zeros((attn_width, model_width), jnp.float32),
    )
    (grad_w_qkv, grad_b_qv, grad_w_out), seq_d = lax.scan(
        backward_seq, start_grads, (seq_input, segment_ids, seq_lse, seq_grad)
    )
    all_d = [gradient.reshape(-1, attn_width) for gradient in seq_d]
    summed = jnp.zeros((my_rows * lax.axis_size("tensor"), model_width), jnp.float32)
    for which in range(3):
        piece = all_d[which]
        summed = summed + jnp.einsum(
            "te,de->td", piece, w_qkv[which], preferred_element_type=jnp.float32
        )
    grad_input = d_first + lax.psum_scatter(
        summed.astype(jnp.bfloat16), "tensor", scatter_dimension=0, tiled=True
    ).astype(jnp.float32)
    grad_w_qkv, grad_b_qv, grad_w_out, grad_w_up, grad_b_up, grad_w_down = (
        lax.psum(grad_w_qkv.astype(jnp.bfloat16), "dp").astype(jnp.float32),
        lax.psum(grad_b_qv.astype(jnp.bfloat16), "dp").astype(jnp.float32),
        lax.psum(grad_w_out.astype(jnp.bfloat16), "dp").astype(jnp.float32),
        lax.psum(grad_w_up.astype(jnp.bfloat16), "dp").astype(jnp.float32),
        lax.psum(grad_b_up.astype(jnp.bfloat16), "dp").astype(jnp.float32),
        lax.psum(grad_w_down.astype(jnp.bfloat16), "dp").astype(jnp.float32),
    )
    grad_b_out, grad_ln1_gain, grad_ln1_bias, grad_b_down, grad_ln2_gain, grad_ln2_bias = lax.psum(
        (grad_b_out, grad_ln1_gain, grad_ln1_bias, grad_b_down, grad_ln2_gain, grad_ln2_bias),
        ("dp", "tensor"),
    )
    return (
        normed_two.astype(jnp.bfloat16),
        grad_input,
        grad_w_qkv,
        grad_b_qv,
        grad_w_out,
        grad_b_out,
        grad_ln1_gain,
        grad_ln1_bias,
        grad_w_up,
        grad_b_up,
        grad_w_down,
        grad_b_down,
        grad_ln2_gain,
        grad_ln2_bias,
    )


def solution(mesh):
    return jax.shard_map(
        local,
        mesh=mesh,
        in_specs=(
            P(("dp", "tensor"), None),
            P("dp", None),
            P(None, None, "tensor"),
            P(None, "tensor"),
            P("tensor", None),
            P(),
            P(),
            P(),
            P(None, "tensor"),
            P("tensor"),
            P("tensor", None),
            P(),
            P(),
            P(),
            P(("dp", "tensor"), None),
        ),
        out_specs=(
            P(("dp", "tensor"), None),
            P(("dp", "tensor"), None),
            P(None, None, "tensor"),
            P(None, "tensor"),
            P("tensor", None),
            P(),
            P(),
            P(),
            P(None, "tensor"),
            P("tensor"),
            P("tensor", None),
            P(),
            P(),
            P(),
        ),
        check_vma=False,
    )
```

profile of v0, /device:TPU:0, one launch (start us, length us, event | category | flops | bytes accessed | tf_op | source)
XLA Modules:
  0.0 977.5 jit_solution(15801574085958323130)
XLA Ops:
  8.0 57.3 %all-gather.5.cloned.1.call-done = bf16[2048,1024]{1,0:T(8,128)(2,1)} async-done(((bf16[512,1024]{1,0:T(8,128)(2,1)}), bf16[2048,1024]{1,0:T(8,128)(2,1)}) %all-gather.5.cloned.1.call-update) | async-done | bytes 4194320 | tf_op jit(solution)/shard_map/all_gather | solution.py:125
  66.4 45.4 %while.33 = (s32[]{:T(128)}, bf16[4,512,256]{2,1,0:T(8,128)(2,1)}, f32[4,4,512,1]{2,1,3,0:T(4,128)S(1)}, bf16[4,512,1024]{2,1,0:T(8,128)(2,1)}, bf16[3,1024,256]...) while((s32[]{:T(128)}, bf16[4,512,256]{2,1,0:T(8,128)(2,1)}, ...), condition=%wide.region_3.4_spmd, body=%wide.region_0.3_spmd.sunk | while | flops 1087371776 | bytes 21310580 | solution.py:140
  111.8 5.8 fusion.111
  118.3 85.9 %reduce-scatter.5.cloned.1.call-done = f32[512,1024]{1,0:T(8,128)} async-done(((f32[2048,1024]{1,0:T(8,128)}), f32[512,1024]{1,0:T(8,128)}) %reduce-scatter.5.cloned.1.call-update) | async-done | bytes 2097168 | tf_op jit(solution)/shard_map/reduce_scatter | solution.py:142
  208.9 52.8 %all-gather.7.cloned.1.call-done = bf16[2048,1024]{1,0:T(8,128)(2,1)} async-done(((bf16[512,1024]{1,0:T(8,128)(2,1)}), bf16[2048,1024]{1,0:T(8,128)(2,1)}) %all-gather.7.cloned.1.call-update) | async-done | bytes 4194320 | tf_op jit(solution)/shard_map/all_gather | solution.py:152
  261.7 8.9 multiply_convert_fusion.1
  272.7 6.6 fusion.112
  280.0 85.9 %reduce-scatter.7.cloned.1.call-done = f32[512,1024]{1,0:T(8,128)} async-done(((f32[2048,1024]{1,0:T(8,128)}), f32[512,1024]{1,0:T(8,128)}) %reduce-scatter.7.cloned.1.call-update) | async-done | bytes 2097168 | tf_op jit(solution)/shard_map/reduce_scatter | solution.py:153
  373.1 52.8 %all-gather.9.cloned.1.call-done = bf16[2048,1024]{1,0:T(8,128)(2,1)} async-done(((bf16[512,1024]{1,0:T(8,128)(2,1)}), bf16[2048,1024]{1,0:T(8,128)(2,1)}) %all-gather.9.cloned.1.call-update) | async-done | bytes 4194320 | tf_op jit(solution)/shard_map/all_gather | solution.py:164
  425.9 11.3 %fusion.109 = (bf16[1024]{0:T(1024)(128)(2,1)S(1)}, bf16[2048,1024]{1,0:T(8,128)(2,1)S(1)}) fusion(f32[2048,1024]{1,0:T(8,128)} %get-tuple-element.268, f32[1024]{0:T(1024)S(1)} %convert_element_type.218, bf16[2048,1024]{1,0:T(8,128)(2,1)} %all-gather.9.cloned.1.call-done, bf16[1024,1024]{1,0:T(8,128)(2,1)} %param.29), kind=kOutput, calls=%fused_computation.164 | convolution fusion | flops 4320132096 | bytes 18880512 | tf_op jit(solution)/shard_map/td,fd->tf/dot_general | solution.py:96
  439.2 7.0 fusion.113
  446.3 86.5 %reduce-scatter.9.cloned.1.call-done = f32[512,1024]{1,0:T(8,128)} async-done(((f32[2048,1024]{1,0:T(8,128)}), f32[512,1024]{1,0:T(8,128)}) %reduce-scatter.9.cloned.1.call-update) | async-done | bytes 2097168 | tf_op jit(solution)/shard_map/reduce_scatter | solution.py:168
  532.8 4.5 multiply_reduce_fusion.1
  539.8 9.5 convolution_convert_fusion.5
  549.3 6.0 convolution_convert_fusion.6
  555.3 37.3 %all-gather.11.cloned.1.call-done = bf16[2048,1024]{1,0:T(8,128)(2,1)} async-done(((bf16[512,1024]{1,0:T(8,128)(2,1)}), bf16[2048,1024]{1,0:T(8,128)(2,1)}) %all-gather.11.cloned.1.call-update) | async-done | bytes 4194320 | tf_op jit(solution)/shard_map/all_gather | solution.py:179
  595.7 172.4 %while.34 = (s32[]{:T(128)}, f32[3,1024,256]{2,1,0:T(8,128)}, f32[2,256]{1,0:T(2,128)S(1)}, f32[256,1024]{1,0:T(8,128)S(1)}, bf16[4,512,256]{2,1,0:T(8,128)(2,1)...) while((s32[]{:T(128)}, f32[3,1024,256]{2,1,0:T(8,128)}, ...), condition=%wide.region_19.20_spmd.clone, body=%wide.region_15.19_spmd.clone.sunk | while | flops 2974292480 | bytes 91798968 | solution.py:246
  614.7 7.1 fusion.236
  621.8 7.3 convert_reduce_fusion.8
  656.4 7.1 fusion.236
  663.5 7.3 convert_reduce_fusion.8
  676.1 4.0 maximum_add_fusion.4
  700.0 7.1 fusion.236
  707.1 7.3 convert_reduce_fusion.8
  719.7 4.0 maximum_add_fusion.4
  743.6 7.1 fusion.236
  750.7 7.3 convert_reduce_fusion.8
  763.2 4.0 maximum_add_fusion.4
  781.3 41.4 %all-reduce = (f32[1024]{0:T(1024)}, f32[1024]{0:T(1024)}, f32[1024]{0:T(1024)}, f32[1024]{0:T(1024)}, f32[1024]{0:T(1024)}, /*index=5*/f32[1024]{0:T(1024)}) all-reduce(f32[1024]{0:T(1024)S(1)} %get-tuple-element.246, f32[1024]{0:T(1024)S(1)} %get-tuple-element.182, ...), channel_id=1, replica_groups=mesh['dp'=8,'tensor'=4] {'dp','tensor'}, use_global_device_ids=true, to_apply=%region_25.26 | all-reduce | flops 6144 | bytes 49152 | tf_op jit(solution)/shard_map/psum | solution.py:267
  822.7 16.7 %all-reduce.1 = (bf16[2,256]{1,0:T(2,128)(2,1)S(1)}, bf16[1024]{0:T(1024)(128)(2,1)S(1)}) all-reduce(bf16[2,256]{1,0:T(2,128)(2,1)S(1)} %convert_element_type.230, bf16[1024]{0:T(1024)(128)(2,1)S(1)} %get-tuple-element.269), channel_id=1, replica_groups=mesh['dp'=8,'tensor'=4] {'dp'}, use_global_device_ids=true, to_apply=%region_22.23 | all-reduce | flops 1536 | bytes 6144 | tf_op jit(solution)/shard_map/psum | solution.py:261
  840.5 70.3 %all-reduce.5.cloned.1.call-done = (bf16[3,1024,256]{2,1,0:T(8,128)(2,1)}, bf16[256,1024]{1,0:T(8,128)(2,1)}, bf16[1024,1024]{1,0:T(8,128)(2,1)}, bf16[1024,1024]{1,0:T(8,128)(2,1)}) async-done(((bf16[3,1024,256]{2,1,0:T(8,128)(2,1)}, bf16[256,1024]{1,0:T(8,128)(2,1)}, bf16[1024,1024]{1,0:T(8,128)(2,1)}, bf16[1024,1024]{1,0:T(8,128)(2,1)}), (bf16[3,1024,256]{2,1,0:T(8,128)(2,1)}, ...) | async-done | bytes 6291472 | tf_op jit(solution)/shard_map/psum | solution.py:260
  921.6 45.3 %reduce-scatter.11.cloned.1.call-done = bf16[512,1024]{1,0:T(8,128)(2,1)} async-done(((bf16[2048,1024]{1,0:T(8,128)(2,1)}), bf16[512,1024]{1,0:T(8,128)(2,1)}) %reduce-scatter.11.cloned.1.call-update) | async-done | bytes 1048592 | tf_op jit(solution)/shard_map/reduce_scatter | solution.py:256
  (324 shorter events, 200.8 us)
Async XLA Ops:
  7.2 254.5 %copy-start = (bf16[1024,1024]{1,0:T(8,128)(2,1)S(1)}, bf16[1024,1024]{1,0:T(8,128)(2,1)}, u32[]{:S(2)}) copy-start(bf16[1024,1024]{1,0:T(8,128)(2,1)} %param.27) | copy-start | bytes 6291460
  7.2 58.1 %all-gather.5.cloned.1.call-start = ((), (), s32[]{:S(2)}) async-start(), calls=%async_computation.4 | async-start | bytes 5242880 | tf_op jit(solution)/shard_map/all_gather | solution.py:125
  7.9 196.3 %reduce-scatter.5.cloned.1.call-start = ((), (), s32[]{:S(2)}) async-start(), calls=%async_computation.5 | async-start | bytes 10485760 | tf_op jit(solution)/shard_map/reduce_scatter | solution.py:142
  117.6 86.6 %copy-start.13 = (bf16[512,1024]{1,0:T(8,128)(2,1)S(1)}, bf16[512,1024]{1,0:T(8,128)(2,1)}, u32[]{:S(2)}) copy-start(bf16[512,1024]{1,0:T(8,128)(2,1)} %param.19) | copy-start | bytes 3145732
  117.6 144.1 %all-gather.7.cloned.1.call-start = ((), (), s32[]{:S(2)}) async-start(), calls=%async_computation.6 | async-start | bytes 5242880 | tf_op jit(solution)/shard_map/all_gather | solution.py:152
  118.3 89.2 %copy-start.18 = (f32[1024]{0:T(1024)S(1)}, f32[1024]{0:T(1024)}, u32[]{:S(2)}) copy-start(f32[1024]{0:T(1024)} %param.25) | copy-start | bytes 12292
  118.3 89.2 %copy-start.22 = (f32[1024]{0:T(1024)S(1)}, f32[1024]{0:T(1024)}, u32[]{:S(2)}) copy-start(f32[1024]{0:T(1024)} %param.26) | copy-start | bytes 12292
  208.9 157.0 %reduce-scatter.7.cloned.1.call-start = ((), (), s32[]{:S(2)}) async-start(), calls=%async_computation.7 | async-start | bytes 10485760 | tf_op jit(solution)/shard_map/reduce_scatter | solution.py:153
  261.7 11.0 %copy-start.29 = (bf16[1024,1024]{1,0:T(8,128)(2,1)S(1)}, bf16[1024,1024]{1,0:T(8,128)(2,1)}, u32[]{:S(2)}) copy-start(bf16[1024,1024]{1,0:T(8,128)(2,1)} %param.29) | copy-start | bytes 6291460
  279.3 146.6 %all-gather.9.cloned.1.call-start = ((), (), s32[]{:S(2)}) async-start(), calls=%async_computation.8 | async-start | bytes 5242880 | tf_op jit(solution)/shard_map/all_gather | solution.py:164
  280.0 89.2 %copy-start.9 = (bf16[512,1024]{1,0:T(8,128)(2,1)S(1)}, bf16[512,1024]{1,0:T(8,128)(2,1)}, u32[]{:S(2)}) copy-start(bf16[512,1024]{1,0:T(8,128)(2,1)} %param.33) | copy-start | bytes 3145732
  280.0 89.3 %copy-start.19 = (f32[1024]{0:T(1024)S(1)}, f32[1024]{0:T(1024)}, u32[]{:S(2)}) copy-start(f32[1024]{0:T(1024)} %param.31) | copy-start | bytes 12292
  373.1 159.7 %reduce-scatter.9.cloned.1.call-start = ((), (), s32[]{:S(2)}) async-start(), calls=%async_computation.9 | async-start | bytes 10485760 | tf_op jit(solution)/shard_map/reduce_scatter | solution.py:168
  446.2 86.6 %copy-start.4 = (f32[512,1024]{1,0:T(8,128)S(1)}, f32[512,1024]{1,0:T(8,128)}, u32[]{:S(2)}) copy-start(f32[512,1024]{1,0:T(8,128)} %copy-done.3) | copy-start | bytes 6291460
  446.2 86.6 %copy-start.24 = (f32[1024]{0:T(1024)S(1)}, f32[1024]{0:T(1024)}, u32[]{:S(2)}) copy-start(f32[1024]{0:T(1024)} %param.32) | copy-start | bytes 12292
  446.3 146.3 %all-gather.11.cloned.1.call-start = ((), (), s32[]{:S(2)}) async-start(), calls=%async_computation.10 | async-start | bytes 5242880 | tf_op jit(solution)/shard_map/all_gather | solution.py:179
  539.7 371.2 %all-reduce.5.cloned.1.call-start = ((), (), s32[]{:S(2)}) async-start(), calls=%async_computation.12 | async-start | bytes 12582912 | tf_op jit(solution)/shard_map/psum | solution.py:260
  539.8 9.5 copy-start.28
  539.8 9.5 copy-start.36
  555.3 40.4 %copy-start.17 = (bf16[2,256]{1,0:T(2,128)(2,1)S(1)}, bf16[2,256]{1,0:T(2,128)(2,1)}, u32[]{:S(2)}) copy-start(bf16[2,256]{1,0:T(2,128)(2,1)} %get-tuple-element.548) | copy-start | bytes 3076
  600.4 5.1 copy-start.32
  610.2 4.5 copy-start.33
  614.7 7.1 copy-start.31
  642.0 5.1 copy-start.32
  656.4 7.1 copy-start.31
  685.6 5.1 copy-start.32
  700.0 7.1 copy-start.31
  729.2 5.1 copy-start.32
  743.6 7.1 copy-start.31
  772.2 194.7 %reduce-scatter.11.cloned.1.call-start = ((), (), s32[]{:S(2)}) async-start(), calls=%async_computation.11 | async-start | bytes 5242880 | tf_op jit(solution)/shard_map/reduce_scatter | solution.py:256
  910.9 5.6 copy-start.15
  919.0 51.6 %copy-start.1 = (bf16[1024,1024]{1,0:T(8,128)(2,1)S(1)}, bf16[1024,1024]{1,0:T(8,128)(2,1)}, u32[]{:S(2)}) copy-start(bf16[1024,1024]{1,0:T(8,128)(2,1)} %param.27) | copy-start | bytes 6291460
  (38 other events, 87.6 us)
Sparse Core Ops, SparseCore 0:
  9.9 55.3 all-gather.4
  117.7 86.4 reduce-scatter.4
  209.0 52.6 all-gather.6
  279.4 86.4 reduce-scatter.6
  373.2 52.6 all-gather.8
  446.4 86.4 reduce-scatter.8
  539.8 52.6 all-gather.10
  772.3 138.4 all-reduce.4
  914.1 52.7 reduce-scatter.10
where the time goes:
time: 988 us; the launch traced here: 978 us
  waiting for transfers between devices  575 us (58%)
  matrix products  230 us (23%)
  other arithmetic  59.9 us (6%)
  blocking collectives  58.1 us (6%)
  local copies, waits for them, and re-layouts  38 us (4%)
  between operations  14.5 us (1%)
    reduce_scatter x1, waiting for transfers between devices, local(): lax.psum_scatter(jnp.einsum('tf,df->td', d_up, w_up, preferred_element_ty...  86.5 us
    reduce_scatter x1, waiting for transfers between devices, local(): lax.psum_scatter(jnp.dot(all_context, w_out, preferred_element_type=jnp.f...  85.9 us
    reduce_scatter x1, waiting for transfers between devices, local(): lax.psum_scatter(ffn_forward(whole_normed, w_up, b_up, w_down), 'tensor',...  85.9 us
    psum x1, waiting for transfers between devices, local(): lax.psum(grad_w_qkv.astype(jnp.bfloat16), 'dp').astype(jnp.float32)  70.3 us
    all_gather x1, waiting for transfers between devices, local(): whole_input = lax.all_gather(layer_input, 'tensor', axis=0, tiled=True)  57.3 us
    all_gather x1, waiting for transfers between devices, local(): whole_branch = lax.all_gather(branch_low, 'tensor', axis=0, tiled=True)  52.8 us
    all_gather x1, waiting for transfers between devices, local(): whole_normed = lax.all_gather(normed_low, 'tensor', axis=0, tiled=True)  52.8 us
    reduce_scatter x1, waiting for transfers between devices, local(): lax.psum_scatter(summed.astype(jnp.bfloat16), 'tensor', scatter_dimension...  45.3 us
  transfers between devices with their start and end apart: 9, of which 9 were waited for; matrix products, arithmetic and copies ran while one was open for 4% of the time, Pallas kernels for 0%

commit v1 on v0

--- a/solution.py
+++ b/solution.py
@@ -257,7 +257,7 @@
         summed.astype(jnp.bfloat16), "tensor", scatter_dimension=0, tiled=True
     ).astype(jnp.float32)
     grad_w_qkv, grad_b_qv, grad_w_out, grad_w_up, grad_b_up, grad_w_down = (
-        lax.psum(grad_w_qkv.astype(jnp.bfloat16), "dp").astype(jnp.float32),
+        jnp.sum(lax.all_gather(grad_w_qkv.astype(jnp.bfloat16), "dp"), axis=0).astype(jnp.float32),
         lax.psum(grad_b_qv.astype(jnp.bfloat16), "dp").astype(jnp.float32),
         lax.psum(grad_w_out.astype(jnp.bfloat16), "dp").astype(jnp.float32),
         lax.psum(grad_w_up.astype(jnp.bfloat16), "dp").astype(jnp.float32),

time: 988 us -> 1080 us (1.093)
  waiting for transfers between devices: 575 us -> 661 us
    all_gather x0 -> x1, waiting for transfers between devices: none -> 115 us  [local(): lax.all_gather(grad_w_qkv.astype(jnp.bfloat16), 'dp')]
    psum x1, waiting for transfers between devices: 70.3 us -> 38.9 us  [local(): lax.psum(grad_w_out.astype(jnp.bfloat16), 'dp').astype(jnp.float32)]
  transfers between devices with their start and end apart: 9 -> 10, of which waited for: 9 -> 10; matrix products, arithmetic and copies ran while one was open for 4% -> 4% of each run, Pallas kernels for 0% -> 0%
where the time goes in v1:
time: 1080 us; the launch traced here: 1070 us
  waiting for transfers between devices  661 us (61%)
  matrix products  230 us (21%)
  other arithmetic  68.7 us (6%)
  blocking collectives  57.3 us (5%)
  local copies, waits for them, and re-layouts  36.6 us (3%)
  between operations  14.9 us (1%)
    all_gather x1, waiting for transfers between devices, local(): lax.all_gather(grad_w_qkv.astype(jnp.bfloat16), 'dp')  115 us
    reduce_scatter x1, waiting for transfers between devices, local(): lax.psum_scatter(jnp.einsum('tf,df->td', d_up, w_up, preferred_element_ty...  86.5 us
    reduce_scatter x1, waiting for transfers between devices, local(): lax.psum_scatter(jnp.dot(all_context, w_out, preferred_element_type=jnp.f...  85.9 us
    reduce_scatter x1, waiting for transfers between devices, local(): lax.psum_scatter(ffn_forward(whole_normed, w_up, b_up, w_down), 'tensor',...  85.9 us
    all_gather x1, waiting for transfers between devices, local(): whole_input = lax.all_gather(layer_input, 'tensor', axis=0, tiled=True)  57.3 us
    all_gather x1, waiting for transfers between devices, local(): whole_branch = lax.all_gather(branch_low, 'tensor', axis=0, tiled=True)  52.8 us
    all_gather x1, waiting for transfers between devices, local(): whole_normed = lax.all_gather(normed_low, 'tensor', axis=0, tiled=True)  52.8 us
    reduce_scatter x1, waiting for transfers between devices, local(): lax.psum_scatter(summed.astype(jnp.bfloat16), 'tensor', scatter_dimension...  47.2 us
  transfers between devices with their start and end apart: 10, of which 10 were waited for; matrix products, arithmetic and copies ran while one was open for 4% of the time, Pallas kernels for 0%

profile of v1, /device:TPU:0, one launch (start us, length us, event | category | flops | bytes accessed | tf_op | source)
XLA Modules:
  0.0 1070.4 jit_solution(2534823326463418211)
XLA Ops:
  8.0 57.3 %all-gather.7.cloned.1.call-done = bf16[2048,1024]{1,0:T(8,128)(2,1)} async-done(((bf16[512,1024]{1,0:T(8,128)(2,1)}), bf16[2048,1024]{1,0:T(8,128)(2,1)}) %all-gather.7.cloned.1.call-update) | async-done | bytes 4194320 | tf_op jit(solution)/shard_map/all_gather | solution.py:125
  66.4 45.4 %while.33 = (s32[]{:T(128)}, bf16[4,512,256]{2,1,0:T(8,128)(2,1)}, f32[4,4,512,1]{2,1,3,0:T(4,128)S(1)}, bf16[4,512,1024]{2,1,0:T(8,128)(2,1)}, bf16[3,1024,256]...) while((s32[]{:T(128)}, bf16[4,512,256]{2,1,0:T(8,128)(2,1)}, ...), condition=%wide.region_3.4_spmd, body=%wide.region_0.3_spmd.sunk | while | flops 1087371776 | bytes 21310580 | solution.py:140
  111.8 5.8 fusion.111
  118.3 85.9 %reduce-scatter.5.cloned.1.call-done = f32[512,1024]{1,0:T(8,128)} async-done(((f32[2048,1024]{1,0:T(8,128)}), f32[512,1024]{1,0:T(8,128)}) %reduce-scatter.5.cloned.1.call-update) | async-done | bytes 2097168 | tf_op jit(solution)/shard_map/reduce_scatter | solution.py:142
  208.9 52.8 %all-gather.9.cloned.1.call-done = bf16[2048,1024]{1,0:T(8,128)(2,1)} async-done(((bf16[512,1024]{1,0:T(8,128)(2,1)}), bf16[2048,1024]{1,0:T(8,128)(2,1)}) %all-gather.9.cloned.1.call-update) | async-done | bytes 4194320 | tf_op jit(solution)/shard_map/all_gather | solution.py:152
  261.7 8.9 multiply_convert_fusion.1
  272.7 6.6 fusion.112
  280.0 85.9 %reduce-scatter.7.cloned.1.call-done = f32[512,1024]{1,0:T(8,128)} async-done(((f32[2048,1024]{1,0:T(8,128)}), f32[512,1024]{1,0:T(8,128)}) %reduce-scatter.7.cloned.1.call-update) | async-done | bytes 2097168 | tf_op jit(solution)/shard_map/reduce_scatter | solution.py:153
  373.1 52.8 %all-gather.11.cloned.1.call-done = bf16[2048,1024]{1,0:T(8,128)(2,1)} async-done(((bf16[512,1024]{1,0:T(8,128)(2,1)}), bf16[2048,1024]{1,0:T(8,128)(2,1)}) %all-gather.11.cloned.1.call-update) | async-done | bytes 4194320 | tf_op jit(solution)/shard_map/all_gather | solution.py:164
  425.9 11.3 %fusion.109 = (bf16[1024]{0:T(1024)(128)(2,1)S(1)}, bf16[2048,1024]{1,0:T(8,128)(2,1)S(1)}) fusion(f32[2048,1024]{1,0:T(8,128)} %get-tuple-element.267, f32[1024]{0:T(1024)S(1)} %convert_element_type.220, bf16[2048,1024]{1,0:T(8,128)(2,1)} %all-gather.11.cloned.1.call-done, bf16[1024,1024]{1,0:T(8,128)(2,1)} %param.29), kind=kOutput, calls=%fused_computation.164 | convolution fusion | flops 4320132096 | bytes 18880512 | tf_op jit(solution)/shard_map/td,fd->tf/dot_general | solution.py:96
  439.2 7.0 fusion.113
  446.3 86.5 %reduce-scatter.9.cloned.1.call-done = f32[512,1024]{1,0:T(8,128)} async-done(((f32[2048,1024]{1,0:T(8,128)}), f32[512,1024]{1,0:T(8,128)}) %reduce-scatter.9.cloned.1.call-update) | async-done | bytes 2097168 | tf_op jit(solution)/shard_map/reduce_scatter | solution.py:168
  532.8 4.5 multiply_reduce_fusion.1
  539.8 9.6 convolution_convert_fusion.5
  549.3 6.0 convolution_convert_fusion.6
  555.4 37.2 %all-gather.13.cloned.1.call-done = bf16[2048,1024]{1,0:T(8,128)(2,1)} async-done(((bf16[512,1024]{1,0:T(8,128)(2,1)}), bf16[2048,1024]{1,0:T(8,128)(2,1)}) %all-gather.13.cloned.1.call-update) | async-done | bytes 4194320 | tf_op jit(solution)/shard_map/all_gather | solution.py:179
  595.7 172.4 %while.34 = (s32[]{:T(128)}, f32[3,1024,256]{2,1,0:T(8,128)}, f32[2,256]{1,0:T(2,128)S(1)}, f32[256,1024]{1,0:T(8,128)S(1)}, bf16[4,512,256]{2,1,0:T(8,128)(2,1)...) while((s32[]{:T(128)}, f32[3,1024,256]{2,1,0:T(8,128)}, ...), condition=%wide.region_19.20_spmd.clone, body=%wide.region_15.19_spmd.clone.sunk | while | flops 2974292480 | bytes 91798968 | solution.py:246
  614.7 7.1 fusion.236
  621.8 7.3 convert_reduce_fusion.8
  656.4 7.1 fusion.236
  663.5 7.3 convert_reduce_fusion.8
  700.0 7.1 fusion.236
  707.1 7.3 convert_reduce_fusion.8
  743.5 7.1 fusion.236
  750.7 7.3 convert_reduce_fusion.8
  780.1 41.5 %all-reduce = (f32[1024]{0:T(1024)}, f32[1024]{0:T(1024)}, f32[1024]{0:T(1024)}, f32[1024]{0:T(1024)}, f32[1024]{0:T(1024)}, /*index=5*/f32[1024]{0:T(1024)}) all-reduce(f32[1024]{0:T(1024)S(1)} %get-tuple-element.245, f32[1024]{0:T(1024)S(1)} %get-tuple-element.182, ...), channel_id=1, replica_groups=mesh['dp'=8,'tensor'=4] {'dp','tensor'}, use_global_device_ids=true, to_apply=%region_25.26 | all-reduce | flops 6144 | bytes 49152 | tf_op jit(solution)/shard_map/psum | solution.py:267
  821.5 15.9 %all-reduce.1 = (bf16[2,256]{1,0:T(2,128)(2,1)S(1)}, bf16[1024]{0:T(1024)(128)(2,1)S(1)}) all-reduce(bf16[2,256]{1,0:T(2,128)(2,1)S(1)} %convert_element_type.232, bf16[1024]{0:T(1024)(128)(2,1)S(1)} %get-tuple-element.268), channel_id=1, replica_groups=mesh['dp'=8,'tensor'=4] {'dp'}, use_global_device_ids=true, to_apply=%region_22.23 | all-reduce | flops 1536 | bytes 6144 | tf_op jit(solution)/shard_map/psum | solution.py:261
  838.6 38.9 %all-reduce.5.cloned.1.call-done = (bf16[256,1024]{1,0:T(8,128)(2,1)}, bf16[1024,1024]{1,0:T(8,128)(2,1)}, bf16[1024,1024]{1,0:T(8,128)(2,1)}) async-done(((bf16[256,1024]{1,0:T(8,128)(2,1)}, bf16[1024,1024]{1,0:T(8,128)(2,1)}, bf16[1024,1024]{1,0:T(8,128)(2,1)}), (bf16[256,1024]{1,0:T(8,128)(2,1)}, bf16[1024,1024]{1,0:T(8,128)(2,1)}, bf16[1024,1024]{1,0:T(8,128)(2,1)})) %all-reduce.5.cloned.1.call-update) | async-done | bytes 4718608 | tf_op jit(solution)/shard_map/psum | solution.py:262
  879.5 4.2 convert_element_type.238
  886.2 47.2 %reduce-scatter.11.cloned.1.call-done = bf16[512,1024]{1,0:T(8,128)(2,1)} async-done(((bf16[2048,1024]{1,0:T(8,128)(2,1)}), bf16[512,1024]{1,0:T(8,128)(2,1)}) %reduce-scatter.11.cloned.1.call-update) | async-done | bytes 1048592 | tf_op jit(solution)/shard_map/reduce_scatter | solution.py:256
  936.4 115.3 %all-gather.15.cloned.1.call-done = bf16[24,1024,256]{2,1,0:T(8,128)(2,1)} async-done(((bf16[3,1024,256]{2,1,0:T(8,128)(2,1)}), bf16[24,1024,256]{2,1,0:T(8,128)(2,1)}) %all-gather.15.cloned.1.call-update) | async-done | bytes 12582928 | tf_op jit(solution)/shard_map/all_gather | solution.py:260
  1051.7 8.0 reduce_sum.194
  (328 shorter events, 208.1 us)
Async XLA Ops:
  7.2 254.5 %copy-start = (bf16[1024,1024]{1,0:T(8,128)(2,1)S(1)}, bf16[1024,1024]{1,0:T(8,128)(2,1)}, u32[]{:S(2)}) copy-start(bf16[1024,1024]{1,0:T(8,128)(2,1)} %param.27) | copy-start | bytes 6291460
  7.2 58.1 %all-gather.7.cloned.1.call-start = ((), (), s32[]{:S(2)}) async-start(), calls=%async_computation.4 | async-start | bytes 5242880 | tf_op jit(solution)/shard_map/all_gather | solution.py:125
  7.9 196.3 %reduce-scatter.5.cloned.1.call-start = ((), (), s32[]{:S(2)}) async-start(), calls=%async_computation.5 | async-start | bytes 10485760 | tf_op jit(solution)/shard_map/reduce_scatter | solution.py:142
  117.6 86.6 %copy-start.14 = (bf16[512,1024]{1,0:T(8,128)(2,1)S(1)}, bf16[512,1024]{1,0:T(8,128)(2,1)}, u32[]{:S(2)}) copy-start(bf16[512,1024]{1,0:T(8,128)(2,1)} %param.19) | copy-start | bytes 3145732
  117.6 144.1 %all-gather.9.cloned.1.call-start = ((), (), s32[]{:S(2)}) async-start(), calls=%async_computation.6 | async-start | bytes 5242880 | tf_op jit(solution)/shard_map/all_gather | solution.py:152
  118.3 89.2 %copy-start.18 = (f32[1024]{0:T(1024)S(1)}, f32[1024]{0:T(1024)}, u32[]{:S(2)}) copy-start(f32[1024]{0:T(1024)} %param.25) | copy-start | bytes 12292
  118.3 89.2 %copy-start.22 = (f32[1024]{0:T(1024)S(1)}, f32[1024]{0:T(1024)}, u32[]{:S(2)}) copy-start(f32[1024]{0:T(1024)} %param.26) | copy-start | bytes 12292
  208.9 157.0 %reduce-scatter.7.cloned.1.call-start = ((), (), s32[]{:S(2)}) async-start(), calls=%async_computation.7 | async-start | bytes 10485760 | tf_op jit(solution)/shard_map/reduce_scatter | solution.py:153
  261.7 11.0 %copy-start.29 = (bf16[1024,1024]{1,0:T(8,128)(2,1)S(1)}, bf16[1024,1024]{1,0:T(8,128)(2,1)}, u32[]{:S(2)}) copy-start(bf16[1024,1024]{1,0:T(8,128)(2,1)} %param.29) | copy-start | bytes 6291460
  279.3 146.6 %all-gather.11.cloned.1.call-start = ((), (), s32[]{:S(2)}) async-start(), calls=%async_computation.8 | async-start | bytes 5242880 | tf_op jit(solution)/shard_map/all_gather | solution.py:164
  280.0 89.2 %copy-start.9 = (bf16[512,1024]{1,0:T(8,128)(2,1)S(1)}, bf16[512,1024]{1,0:T(8,128)(2,1)}, u32[]{:S(2)}) copy-start(bf16[512,1024]{1,0:T(8,128)(2,1)} %param.33) | copy-start | bytes 3145732
  280.0 89.3 %copy-start.19 = (f32[1024]{0:T(1024)S(1)}, f32[1024]{0:T(1024)}, u32[]{:S(2)}) copy-start(f32[1024]{0:T(1024)} %param.31) | copy-start | bytes 12292
  373.1 159.7 %reduce-scatter.9.cloned.1.call-start = ((), (), s32[]{:S(2)}) async-start(), calls=%async_computation.9 | async-start | bytes 10485760 | tf_op jit(solution)/shard_map/reduce_scatter | solution.py:168
  446.2 86.6 %copy-start.4 = (f32[512,1024]{1,0:T(8,128)S(1)}, f32[512,1024]{1,0:T(8,128)}, u32[]{:S(2)}) copy-start(f32[512,1024]{1,0:T(8,128)} %copy-done.3) | copy-start | bytes 6291460
  446.2 86.6 %copy-start.24 = (f32[1024]{0:T(1024)S(1)}, f32[1024]{0:T(1024)}, u32[]{:S(2)}) copy-start(f32[1024]{0:T(1024)} %param.32) | copy-start | bytes 12292
  446.3 146.3 %all-gather.13.cloned.1.call-start = ((), (), s32[]{:S(2)}) async-start(), calls=%async_computation.10 | async-start | bytes 5242880 | tf_op jit(solution)/shard_map/all_gather | solution.py:179
  539.7 337.7 %all-reduce.5.cloned.1.call-start = ((), (), s32[]{:S(2)}) async-start(), calls=%async_computation.13 | async-start | bytes 9437184 | tf_op jit(solution)/shard_map/psum | solution.py:262
  539.8 9.6 copy-start.28
  539.8 9.6 copy-start.36
  555.4 40.3 %copy-start.17 = (bf16[2,256]{1,0:T(2,128)(2,1)S(1)}, bf16[2,256]{1,0:T(2,128)(2,1)}, u32[]{:S(2)}) copy-start(bf16[2,256]{1,0:T(2,128)(2,1)} %get-tuple-element.547) | copy-start | bytes 3076
  600.3 5.1 copy-start.32
  614.7 7.1 copy-start.31
  642.0 5.1 copy-start.32
  656.4 7.1 copy-start.31
  685.6 5.1 copy-start.32
  700.0 7.1 copy-start.31
  729.2 5.1 copy-start.32
  743.5 7.1 copy-start.31
  769.0 164.5 %reduce-scatter.11.cloned.1.call-start = ((), (), s32[]{:S(2)}) async-start(), calls=%async_computation.11 | async-start | bytes 5242880 | tf_op jit(solution)/shard_map/reduce_scatter | solution.py:256
  776.7 275.0 %all-gather.15.cloned.1.call-start = ((), (), s32[]{:S(2)}) async-start(), calls=%async_computation.12 | async-start | bytes 14155776 | tf_op jit(solution)/shard_map/all_gather | solution.py:260
  883.8 49.7 %copy-start.10 = (f32[512,1024]{1,0:T(8,128)S(1)}, f32[512,1024]{1,0:T(8,128)}, u32[]{:S(2)}) copy-start(f32[512,1024]{1,0:T(8,128)} %get-tuple-element.247) | copy-start | bytes 6291460
  1051.7 11.4 %copy-start.1 = (bf16[1024,1024]{1,0:T(8,128)(2,1)S(1)}, bf16[1024,1024]{1,0:T(8,128)(2,1)}, u32[]{:S(2)}) copy-start(bf16[1024,1024]{1,0:T(8,128)(2,1)} %param.27) | copy-start | bytes 6291460
  (39 other events, 101.8 us)
Sparse Core Ops, SparseCore 0:
  9.9 55.3 all-gather.6
  117.7 86.4 reduce-scatter.4
  209.0 52.6 all-gather.8
  279.4 86.4 reduce-scatter.6
  373.2 52.6 all-gather.10
  446.4 86.4 reduce-scatter.8
  539.8 52.6 all-gather.12
  769.1 108.2 all-reduce.4
  880.7 52.7 reduce-scatter.10
  935.0 116.7 all-gather.14
